TPU v7x, 32 devices: a whole 2x2x4 slice. The times are simulated.
32 devices in a mesh: row: 8 (over z, y), col: 4 (over x, core).
Axes of the slice: x: 2, y: 2, z: 4, core: 2. Of those that a mesh axis runs over, the one named last changes fastest.
Arguments:
- trail_adjoint: float32 [4096, 4096], P('row', 'col'), may hold values from -6 to 6
- lower_new: float32 [4096, 256], P('row', 'col'), may hold values from -0.09375 to 0.09375
- upper_new: float32 [256, 4096], P('row', 'col'), may hold values from -0.09375 to 0.09375
- lower_old_top: float32 [256, 256], replicated, may hold values from -0.375 to 0.375
- lower_old: float32 [4096, 256], P('row', 'col'), may hold values from -0.09375 to 0.09375
- upper_old_left: float32 [256, 256], replicated, may hold values from -0.375 to 0.375
- upper_old: float32 [256, 4096], P('row', 'col'), may hold values from -0.09375 to 0.09375
- diag_lower_new: float32 [256, 256], replicated, as said below
- diag_upper_new: float32 [256, 256], replicated, as said below
- inverse_lower_new: float32 [256, 256], replicated, as said below
- inverse_upper_new: float32 [256, 256], replicated, as said below
- diag_lower_old: float32 [256, 256], replicated, as said below
- diag_upper_old: float32 [256, 256], replicated, as said below
- inverse_lower_old: float32 [256, 256], replicated, as said below
- inverse_upper_old: float32 [256, 256], replicated, as said below
Outputs:
- corner_old: float32 [256, 256], replicated
- strip_top: float32 [256, 256], replicated
- strip_bottom: float32 [4096, 256], P(('row', 'col'))
- band_left: float32 [256, 256], replicated
- band_right: float32 [256, 4096], P(None, 'col')
Inputs may be any that keep to these rules, and one draw needn't show every extreme that they name: `diag_lower_new`: unit lower triangular. `diag_upper_new`: upper triangular, diagonal from 1 to 2. `inverse_lower_new`: the inverse of diag_lower_new. `inverse_upper_new`: the inverse of diag_upper_new. `diag_lower_old`: unit lower triangular. `diag_upper_old`: upper triangular, diagonal from 1 to 2. `inverse_lower_old`: the inverse of diag_lower_old. `inverse_upper_old`: the inverse of diag_upper_old.
All inputs are finite; a program needn't handle non-finite values.
Results may differ from a plain program's by a relative error of at most 0.000075.
Values sent between devices are 32-bit elements; how exact they have to be, the bound alone decides.
A program may use at most 128 MiB of HBM per device.

v0:
```python
import jax
import jax.numpy as jnp
from jax import lax
from jax.sharding import PartitionSpec as P

precise = lax.Precision.HIGH


def dot(left, right, a, b):
    return lax.dot_general(left, right, (((a,), (b,)), ((), ())), precision=precise)


def body(an, ln, un, lot, lo, uol, uo, dln, dun, iln, iun, dlo, duo, ilo, iuo):
    width = iln.shape[0]
    uppers = lax.all_gather(jnp.concatenate((un[None], uo[None])), "row", axis=1, tiled=True)
    lowers = lax.all_gather(jnp.concatenate((ln[None], lo[None])), "col", axis=2, tiled=True)
    un, uo = (uppers[0], uppers[1])
    ln, lo = (lowers[0], lowers[1])
    mix_u = dot(dot(iuo, uol, 1, 0), iun, 1, 0)
    mix_l = dot(dot(iln, lot, 1, 0), ilo, 1, 0)
    ut = dot(iuo, uo, 1, 0) - dot(mix_u, un, 1, 0)
    lt = dot(lo, ilo, 1, 0) - dot(ln, mix_l, 1, 0)
    strip = -dot(an, ut, 1, 1)
    band = -dot(lt, an, 0, 0)
    left = -dot(band, un, 1, 1)
    both = -dot(jnp.concatenate((ln, lt), axis=1), strip, 0, 0)
    small = lax.psum(jnp.concatenate((left, both), axis=0), ("row", "col"))
    strip = lax.psum_scatter(strip, "col", scatter_dimension=0, tiled=True)
    band = lax.psum(band, "row")
    band_left = dot(small[:width], iun, 1, 1)
    strip_top = dot(iln, small[width : 2 * width], 0, 0)
    corner = small[2 * width :]
    return (corner, strip_top, strip, band_left, band)


def solution(mesh):
    split, whole = (P("row", "col"), P())
    return jax.shard_map(
        body,
        mesh=mesh,
        in_specs=(split, split, split, whole, split, whole, split) + (whole,) * 8,
        out_specs=(P(), P(), P(("row", "col"), None), P(), P(None, "col")),
        check_vma=False,
    )
```

profile of v0, /device:TPU:0, one launch (start us, length us, event | category | flops | bytes accessed | tf_op | source)
XLA Modules:
  0.0 331.9 jit_solution(3750939363003081247)
XLA Ops:
  7.2 0.0 copy-start
  7.2 0.0 copy-start.8
  7.2 0.0 copy-start.11
  7.2 0.0 copy-start.13
  7.2 0.0 copy-start.10
  7.2 0.0 all-gather.3.cloned.1.call-start
  7.3 1.8 pad_maximum_fusion.1
  9.1 0.0 all-gather.3.cloned.1.call-update
  9.1 0.0 all-gather.5.cloned.1.call-start
  9.2 1.7 pad_maximum_fusion.2
  10.9 0.0 all-gather.5.cloned.1.call-update
  10.9 0.0 all-reduce.3.cloned.1.call-start
  10.9 1.3 fusion.10
  12.3 0.0 copy-done.8
  12.3 0.3 fusion.11
  12.5 0.0 copy-done.11
  12.6 0.0 copy-done.13
  12.6 0.3 fusion.12
  12.8 0.0 copy-done.10
  12.9 1.0 fusion.13
  13.8 15.8 %all-gather.3.cloned.1.call-done = f32[2,512,256]{1,2,0:T(8,128)} async-done(((f32[2,512,64]{1,2,0:T(8,128)}), f32[2,512,256]{1,2,0:T(8,128)}) %all-gather.3.cloned.1.call-update) | async-done | bytes 1048592 | tf_op jit(solution)/shard_map/all_gather | solution.py:16
  29.6 0.0 copy-start.6
  29.6 2.0 slice_bitcast_fusion.5
  31.6 1.5 fusion.5
  33.1 0.0 copy-done.6
  33.1 0.5 convolution_subtract_fusion
  33.5 0.0 copy-start.2
  33.5 0.8 copy-done.2
  34.3 0.0 copy-done
  34.3 1.1 convolution_negate_fusion
  35.4 0.0 copy-start.1
  35.4 46.1 %all-gather.5.cloned.1.call-done = f32[2,256,1024]{2,1,0:T(8,128)} async-done(((f32[2,32,1024]{2,1,0:T(8,128)}), f32[2,256,1024]{2,1,0:T(8,128)}) %all-gather.5.cloned.1.call-update) | async-done | bytes 2097168 | tf_op jit(solution)/shard_map/all_gather | solution.py:15
  81.5 0.0 copy-start.4
  81.5 2.5 fusion.4
  84.0 0.0 copy-done.4
  84.0 0.0 copy-done.12
  84.0 1.0 fusion
  85.0 0.0 copy-start.3
  85.0 0.0 copy-start.7
  85.0 1.9 convolution_negate_fusion.2
  87.0 0.0 copy-done.3
  87.0 0.0 copy-done.7
  87.0 0.0 copy-start.5
  87.0 0.6 convolution_negate_fusion.1
  87.6 0.0 copy-done.1
  87.6 0.7 convolution_negate_fusion.3
  88.3 0.0 copy-done.5
  88.3 0.0 copy-start.9
  88.3 0.9 pad_maximum_fusion
  89.3 0.0 all-reduce.3.cloned.1.call-update
  89.3 0.0 reduce-scatter.2.cloned.1.call-start
  89.3 0.5 reduce-scatter.2.cloned.1.call-update
  89.9 0.0 all-reduce.5.cloned.1.call-start
  89.9 0.5 all-reduce.5.cloned.1.call-update
  90.5 127.4 %all-reduce.3.cloned.1.call-done = f32[768,256]{1,0:T(8,128)} async-done(((f32[768,256]{1,0:T(8,128)}), f32[768,256]{1,0:T(8,128)}) %all-reduce.3.cloned.1.call-update) | async-done | bytes 786448 | tf_op jit(solution)/shard_map/psum | solution.py:27
  217.9 0.0 copy-done.9
  217.9 1.3 convolution_bitcast_fusion.1
  219.2 0.8 copy.16
  220.1 1.7 slice.32
  221.7 2.0 fusion.6
  223.7 17.2 %reduce-scatter.2.cloned.1.call-done = f32[128,256]{0,1:T(8,128)} async-done(((f32[512,256]{0,1:T(8,128)}), f32[128,256]{0,1:T(8,128)}) %reduce-scatter.2.cloned.1.call-update) | async-done | bytes 131088 | tf_op jit(solution)/shard_map/reduce_scatter | solution.py:28
  240.9 1.7 copy.17
  242.6 80.5 %all-reduce.5.cloned.1.call-done = f32[256,1024]{1,0:T(8,128)} async-done(((f32[256,1024]{1,0:T(8,128)}), f32[256,1024]{1,0:T(8,128)}) %all-reduce.5.cloned.1.call-update) | async-done | bytes 1048592 | tf_op jit(solution)/shard_map/psum | solution.py:29
  323.1 2.3 copy.20
  (1 shorter events, 0.0 us)
Async XLA Ops:
  7.2 27.2 %copy-start = (f32[512,1024]{1,0:T(8,128)S(1)}, f32[512,1024]{1,0:T(8,128)}, u32[]{:S(2)}) copy-start(f32[512,1024]{1,0:T(8,128)} %param.15) | copy-start | bytes 6291460
  7.2 5.1 %copy-start.8 = (f32[256,256]{1,0:T(8,128)S(1)}, f32[256,256]{1,0:T(8,128)}, u32[]{:S(2)}) copy-start(f32[256,256]{1,0:T(8,128)} %param.24) | copy-start | bytes 786436
  7.2 5.4 %copy-start.11 = (f32[256,256]{1,0:T(8,128)S(1)}, f32[256,256]{1,0:T(8,128)}, u32[]{:S(2)}) copy-start(f32[256,256]{1,0:T(8,128)} %param.25) | copy-start | bytes 786436
  7.2 5.4 %copy-start.13 = (f32[256,256]{1,0:T(8,128)S(1)}, f32[256,256]{1,0:T(8,128)}, u32[]{:S(2)}) copy-start(f32[256,256]{1,0:T(8,128)} %param.20) | copy-start | bytes 786436
  7.2 5.6 %copy-start.10 = (f32[256,256]{1,0:T(8,128)S(1)}, f32[256,256]{1,0:T(8,128)}, u32[]{:S(2)}) copy-start(f32[256,256]{1,0:T(8,128)} %param.23) | copy-start | bytes 786436
  7.2 22.4 %all-gather.3.cloned.1.call-start = ((), (), s32[]{:S(2)}) async-start(), calls=%async_computation.1 | async-start | bytes 1310720 | tf_op jit(solution)/shard_map/all_gather | solution.py:16
  9.1 72.4 %all-gather.5.cloned.1.call-start = ((), (), s32[]{:S(2)}) async-start(), calls=%async_computation.2 | async-start | bytes 2359296 | tf_op jit(solution)/shard_map/all_gather | solution.py:15
  10.9 207.0 %all-reduce.3.cloned.1.call-start = ((), (), s32[]{:S(2)}) async-start(), calls=%async_computation.3 | async-start | bytes 1572864 | tf_op jit(solution)/shard_map/psum | solution.py:27
  29.6 3.4 %copy-start.6 = (f32[2,512,256]{1,2,0:T(8,128)S(1)}, f32[2,512,256]{1,2,0:T(8,128)}, u32[]{:S(2)}) copy-start(f32[2,512,256]{1,2,0:T(8,128)} %all-gather.3.cloned.1.call-done) | copy-start | bytes 3145732
  33.5 0.8 copy-start.2
  35.4 52.2 %copy-start.1 = (f32[256,1024]{1,0:T(8,128)}, f32[256,1024]{1,0:T(8,128)S(1)}, u32[]{:S(2)}) copy-start(f32[256,1024]{1,0:T(8,128)S(1)} %convolution_negate_fusion) | copy-start | bytes 3145732
  81.5 2.5 copy-start.4
  81.5 2.5 copy-start.12
  85.0 2.0 copy-start.3
  85.0 2.0 copy-start.7
  87.0 1.3 copy-start.5
  88.3 129.6 %copy-start.9 = (f32[256,256]{1,0:T(8,128)S(1)}, f32[256,256]{1,0:T(8,128)}, u32[]{:S(2)}) copy-start(f32[256,256]{1,0:T(8,128)} %param.22) | copy-start | bytes 786436
  89.3 151.6 %reduce-scatter.2.cloned.1.call-start = ((), (), s32[]{:S(2)}) async-start(), calls=%async_computation.4 | async-start | bytes 655360 | tf_op jit(solution)/shard_map/reduce_scatter | solution.py:28
  89.9 233.2 %all-reduce.5.cloned.1.call-start = ((), (), s32[]{:S(2)}) async-start(), calls=%async_computation.5 | async-start | bytes 2097152 | tf_op jit(solution)/shard_map/psum | solution.py:29
Sparse Core Ops, SparseCore 0:
  10.2 19.4 all-gather.2
  32.4 49.0 all-gather.4
  89.4 128.4 all-reduce.2
  220.2 20.6 reduce-scatter.1
  244.8 78.1 all-reduce.4
where the time goes:
time: 332 us
  waiting for transfers between devices  288 us (87%)
  matrix products  15.8 us (5%)
  between operations  14 us (4%)
  local copies, waits for them, and re-layouts  9.28 us (3%)
  other arithmetic  4.48 us (1%)
    psum x1, waiting for transfers between devices, body(): small = lax.psum(jnp.concatenate((left, both), axis=0), ('row', 'col'))  127 us
    psum x1, waiting for transfers between devices, body(): band = lax.psum(band, 'row')  80.5 us
    all_gather x1, waiting for transfers between devices, body(): lax.all_gather(jnp.concatenate((un[None], uo[None])), 'row', axis=1, tile...  46.1 us
    reduce_scatter x1, waiting for transfers between devices, body(): strip = lax.psum_scatter(strip, 'col', scatter_dimension=0, tiled=True)  17.2 us
    dot_general x14, matrix products, dot(): lax.dot_general(left, right, (((a,), (b,)), ((), ())), precision=precise)  15.8 us
    all_gather x1, waiting for transfers between devices, body(): lax.all_gather(jnp.concatenate((ln[None], lo[None])), 'col', axis=2, tile...  15.8 us
  transfers between devices with their start and end apart: 5, of which 5 were waited for; matrix products, arithmetic and copies ran while one was open for 5% of the time, Pallas kernels for 0%

commit v1 on v0

--- a/solution.py
+++ b/solution.py
@@ -26,7 +26,7 @@
     both = -dot(jnp.concatenate((ln, lt), axis=1), strip, 0, 0)
     small = lax.psum(jnp.concatenate((left, both), axis=0), ("row", "col"))
     strip = lax.psum_scatter(strip, "col", scatter_dimension=0, tiled=True)
-    band = lax.psum(band, "row")
+    band = jnp.sum(lax.all_gather(band, "row"), axis=0)
     band_left = dot(small[:width], iun, 1, 1)
     strip_top = dot(iln, small[width : 2 * width], 0, 0)
     corner = small[2 * width :]

time: 332 us -> 380 us (1.14)
  waiting for transfers between devices: 288 us -> 333 us
  other arithmetic: 4.48 us -> 9.8 us
    all_gather x0 -> x1, waiting for transfers between devices: none -> 125 us  [body(): band = jnp.sum(lax.all_gather(band, 'row'), axis=0)]
    psum x1 -> x0, waiting for transfers between devices: 80.5 us -> none  [body(): band = lax.psum(band, 'row')]
    reduce_sum x0 -> x1, other arithmetic: none -> 5.35 us  [body(): band = jnp.sum(lax.all_gather(band, 'row'), axis=0)]
  transfers between devices with their start and end apart: 5 -> 5, of which waited for: 5 -> 5; matrix products, arithmetic and copies ran while one was open for 5% -> 4% of each run, Pallas kernels for 0% -> 0%
where the time goes in v1:
time: 380 us
  waiting for transfers between devices  333 us (88%)
  matrix products  15.8 us (4%)
  between operations  14 us (4%)
  other arithmetic  9.8 us (3%)
  local copies, waits for them, and re-layouts  6.97 us (2%)
    psum x1, waiting for transfers between devices, body(): small = lax.psum(jnp.concatenate((left, both), axis=0), ('row', 'col'))  127 us
    all_gather x1, waiting for transfers between devices, body(): band = jnp.sum(lax.all_gather(band, 'row'), axis=0)  125 us
    all_gather x1, waiting for transfers between devices, body(): lax.all_gather(jnp.concatenate((un[None], uo[None])), 'row', axis=1, tile...  46.1 us
    reduce_scatter x1, waiting for transfers between devices, body(): strip = lax.psum_scatter(strip, 'col', scatter_dimension=0, tiled=True)  17.2 us
    dot_general x14, matrix products, dot(): lax.dot_general(left, right, (((a,), (b,)), ((), ())), precision=precise)  15.8 us
    all_gather x1, waiting for transfers between devices, body(): lax.all_gather(jnp.concatenate((ln[None], lo[None])), 'col', axis=2, tile...  15.8 us
  transfers between devices with their start and end apart: 5, of which 5 were waited for; matrix products, arithmetic and copies ran while one was open for 4% of the time, Pallas kernels for 0%

profile of v1, /device:TPU:0, one launch (start us, length us, event | category | flops | bytes accessed | tf_op | source)
XLA Modules:
  0.0 379.8 jit_solution(1093901752198425080)
XLA Ops:
  7.2 0.0 copy-start
  7.2 0.0 copy-start.8
  7.2 0.0 copy-start.11
  7.2 0.0 copy-start.13
  7.2 0.0 copy-start.10
  7.2 0.0 all-gather.5.cloned.1.call-start
  7.3 1.8 pad_maximum_fusion.1
  9.1 0.0 all-gather.5.cloned.1.call-update
  9.1 0.0 all-gather.7.cloned.1.call-start
  9.2 1.7 pad_maximum_fusion.2
  10.9 0.0 all-gather.7.cloned.1.call-update
  10.9 0.0 all-reduce.2.cloned.1.call-start
  10.9 1.3 fusion.10
  12.3 0.0 copy-done.8
  12.3 0.3 fusion.11
  12.5 0.0 copy-done.11
  12.6 0.0 copy-done.13
  12.6 0.3 fusion.12
  12.8 0.0 copy-done.10
  12.9 1.0 fusion.13
  13.8 15.8 %all-gather.5.cloned.1.call-done = f32[2,512,256]{1,2,0:T(8,128)} async-done(((f32[2,512,64]{1,2,0:T(8,128)}), f32[2,512,256]{1,2,0:T(8,128)}) %all-gather.5.cloned.1.call-update) | async-done | bytes 1048592 | tf_op jit(solution)/shard_map/all_gather | solution.py:16
  29.6 0.0 copy-start.6
  29.6 2.0 slice_bitcast_fusion.5
  31.6 1.5 fusion.5
  33.1 0.0 copy-done.6
  33.1 0.5 convolution_subtract_fusion
  33.5 0.0 copy-start.2
  33.5 0.8 copy-done.2
  34.3 0.0 copy-done
  34.3 1.1 convolution_negate_fusion
  35.4 0.0 copy-start.1
  35.4 46.1 %all-gather.7.cloned.1.call-done = f32[2,256,1024]{2,1,0:T(8,128)} async-done(((f32[2,32,1024]{2,1,0:T(8,128)}), f32[2,256,1024]{2,1,0:T(8,128)}) %all-gather.7.cloned.1.call-update) | async-done | bytes 2097168 | tf_op jit(solution)/shard_map/all_gather | solution.py:15
  81.5 0.0 copy-start.4
  81.5 2.5 fusion.4
  84.0 0.0 copy-done.4
  84.0 0.0 copy-done.12
  84.0 1.0 fusion
  85.0 0.0 copy-start.3
  85.0 0.0 copy-start.7
  85.0 1.9 convolution_negate_fusion.2
  87.0 0.0 copy-done.3
  87.0 0.0 copy-done.7
  87.0 0.0 copy-start.5
  87.0 0.6 convolution_negate_fusion.1
  87.6 0.0 copy-done.1
  87.6 0.7 convolution_negate_fusion.3
  88.3 0.0 copy-done.5
  88.3 0.0 copy-start.9
  88.3 0.9 pad_maximum_fusion
  89.3 0.0 all-reduce.2.cloned.1.call-update
  89.3 0.0 reduce-scatter.2.cloned.1.call-start
  89.3 0.5 reduce-scatter.2.cloned.1.call-update
  89.9 0.0 all-gather.9.cloned.1.call-start
  89.9 0.5 all-gather.9.cloned.1.call-update
  90.4 127.4 %all-reduce.2.cloned.1.call-done = f32[768,256]{1,0:T(8,128)} async-done(((f32[768,256]{1,0:T(8,128)}), f32[768,256]{1,0:T(8,128)}) %all-reduce.2.cloned.1.call-update) | async-done | bytes 786448 | tf_op jit(solution)/shard_map/psum | solution.py:27
  217.9 0.0 copy-done.9
  217.9 1.3 convolution_bitcast_fusion.1
  219.2 0.8 copy.16
  220.0 1.7 slice.32
  221.7 2.0 fusion.6
  223.7 17.2 %reduce-scatter.2.cloned.1.call-done = f32[128,256]{0,1:T(8,128)} async-done(((f32[512,256]{0,1:T(8,128)}), f32[128,256]{0,1:T(8,128)}) %reduce-scatter.2.cloned.1.call-update) | async-done | bytes 131088 | tf_op jit(solution)/shard_map/reduce_scatter | solution.py:28
  240.9 1.7 copy.17
  242.5 125.4 %all-gather.9.cloned.1.call-done = f32[2048,1024]{1,0:T(8,128)} async-done(((f32[256,1024]{1,0:T(8,128)}), f32[2048,1024]{1,0:T(8,128)}) %all-gather.9.cloned.1.call-update) | async-done | bytes 8388624 | tf_op jit(solution)/shard_map/all_gather | solution.py:29
  368.0 5.3 %reduce_sum.9 = f32[256,1024]{1,0:T(8,128)} reduce(f32[8,256,1024]{2,1,0:T(8,128)} %bitcast.45, f32[]{:T(128)} %constant.0.clone.1), dimensions={0}, to_apply=%region_2.0 | reduce | flops 1835008 | bytes 9437188 | tf_op jit(solution)/shard_map/reduce_sum | solution.py:29
  (1 shorter events, 0.0 us)
Async XLA Ops:
  7.2 27.2 %copy-start = (f32[512,1024]{1,0:T(8,128)S(1)}, f32[512,1024]{1,0:T(8,128)}, u32[]{:S(2)}) copy-start(f32[512,1024]{1,0:T(8,128)} %param.15) | copy-start | bytes 6291460
  7.2 5.1 %copy-start.8 = (f32[256,256]{1,0:T(8,128)S(1)}, f32[256,256]{1,0:T(8,128)}, u32[]{:S(2)}) copy-start(f32[256,256]{1,0:T(8,128)} %param.24) | copy-start | bytes 786436
  7.2 5.4 %copy-start.11 = (f32[256,256]{1,0:T(8,128)S(1)}, f32[256,256]{1,0:T(8,128)}, u32[]{:S(2)}) copy-start(f32[256,256]{1,0:T(8,128)} %param.25) | copy-start | bytes 786436
  7.2 5.4 %copy-start.13 = (f32[256,256]{1,0:T(8,128)S(1)}, f32[256,256]{1,0:T(8,128)}, u32[]{:S(2)}) copy-start(f32[256,256]{1,0:T(8,128)} %param.20) | copy-start | bytes 786436
  7.2 5.6 %copy-start.10 = (f32[256,256]{1,0:T(8,128)S(1)}, f32[256,256]{1,0:T(8,128)}, u32[]{:S(2)}) copy-start(f32[256,256]{1,0:T(8,128)} %param.23) | copy-start | bytes 786436
  7.2 22.4 %all-gather.5.cloned.1.call-start = ((), (), s32[]{:S(2)}) async-start(), calls=%async_computation.1 | async-start | bytes 1310720 | tf_op jit(solution)/shard_map/all_gather | solution.py:16
  9.1 72.4 %all-gather.7.cloned.1.call-start = ((), (), s32[]{:S(2)}) async-start(), calls=%async_computation.2 | async-start | bytes 2359296 | tf_op jit(solution)/shard_map/all_gather | solution.py:15
  10.9 207.0 %all-reduce.2.cloned.1.call-start = ((), (), s32[]{:S(2)}) async-start(), calls=%async_computation.3 | async-start | bytes 1572864 | tf_op jit(solution)/shard_map/psum | solution.py:27
  29.6 3.4 copy-start.6
  33.5 0.8 copy-start.2
  35.4 52.2 %copy-start.1 = (f32[256,1024]{1,0:T(8,128)}, f32[256,1024]{1,0:T(8,128)S(1)}, u32[]{:S(2)}) copy-start(f32[256,1024]{1,0:T(8,128)S(1)} %convolution_negate_fusion) | copy-start | bytes 3145732
  81.5 2.5 copy-start.4
  81.5 2.5 copy-start.12
  85.0 2.0 copy-start.3
  85.0 2.0 copy-start.7
  87.0 1.3 copy-start.5
  88.3 129.5 %copy-start.9 = (f32[256,256]{1,0:T(8,128)S(1)}, f32[256,256]{1,0:T(8,128)}, u32[]{:S(2)}) copy-start(f32[256,256]{1,0:T(8,128)} %param.22) | copy-start | bytes 786436
  89.3 151.6 %reduce-scatter.2.cloned.1.call-start = ((), (), s32[]{:S(2)}) async-start(), calls=%async_computation.4 | async-start | bytes 655360 | tf_op jit(solution)/shard_map/reduce_scatter | solution.py:28
  89.9 278.1 %all-gather.9.cloned.1.call-start = ((), (), s32[]{:S(2)}) async-start(), calls=%async_computation.5 | async-start | bytes 9437184 | tf_op jit(solution)/shard_map/all_gather | solution.py:29
Sparse Core Ops, SparseCore 0:
  10.2 19.4 all-gather.4
  32.4 49.0 all-gather.6
  89.4 128.4 all-reduce.1
  220.2 20.6 reduce-scatter.1
  243.4 124.4 all-gather.8
